TPU v7x, 256 devices: a whole 4x4x8 slice. The times are simulated.
256 devices in a mesh: rows: 64 (over z, x, core), cols: 4 (over y).
Axes of the slice: x: 4, y: 4, z: 8, core: 2. Of those that a mesh axis runs over, the one named last changes fastest.
Arguments:
- pass_rates: float32 [32, 1048576], P(None, 'rows'), may hold values from 0 to 1
- upper_blocks: bfloat16 [8192, 8, 128, 128], P('rows', 'cols'), may hold values from 9.9658966e-05 to 0.0099487305
- neighbours: int32 [8192, 8], P('rows', 'cols'), may hold values from 0 to 8191, as said below
Outputs:
- solution: float32 [32, 1048576], P('cols', 'rows')
- residual: float32 [32, 1048576], P('cols', 'rows')
Inputs may be any that keep to these rules, and one draw needn't show every extreme that they name: `neighbours`: slot 0 of block-row b names b itself; every other slot of block-row b names a block from b to b + 256 that exists; in the last block-row of every shard of 128 block-rows, slot 1 names the farthest such block.
All inputs are finite; a program needn't handle non-finite values.
Results may differ from a plain program's by a relative error of at most 0.034.
Values may be sent and summed in bfloat16 or wider, within the bound.
A program may use at most 128 MiB of HBM per device.

v0:
```python
import jax
import jax.numpy as jnp
from jax import lax
from jax.sharding import PartitionSpec as P

REACH = 2
ITERS = 2


def from_behind(value, axis, steps):
    count = lax.axis_size(axis)
    initial, last = (max(0, -steps), min(count, count - steps))
    return lax.ppermute(value, axis, [(source, source + steps) for source in range(initial, last)])


def per_device(pass_rates, upper_blocks, neighbours):
    shard_rows = upper_blocks.shape[0]
    block_width = upper_blocks.shape[2]
    columns = pass_rates.shape[0]
    first_block = lax.axis_index("rows") * shard_rows
    local_index = neighbours - first_block
    own_weight = jnp.sum(upper_blocks, axis=(1, 3), dtype=jnp.float32)
    col_weight = jnp.sum(upper_blocks, axis=2, dtype=jnp.float32)
    share = columns // lax.axis_size("cols")
    residual = pass_rates

    def squares(values):
        return lax.psum(jnp.sum(values * values, axis=1), "rows")

    solution = jnp.zeros_like(residual)
    direction = residual
    norm_now = squares(residual)
    for iteration in range(ITERS):
        rounded = direction.astype(jnp.bfloat16)
        pieces = [rounded]
        for distance in range(1, REACH + 1):
            pieces.append(from_behind(rounded, "rows", -distance))
        window = jnp.concatenate(pieces, axis=1).reshape(
            columns, (REACH + 1) * shard_rows, block_width
        )
        own_block = rounded.reshape(columns, shard_rows, block_width)
        far_blocks = jnp.take(window, local_index, axis=1)
        forward = own_block.astype(jnp.float32) * own_weight[None] - jnp.einsum(
            "bkij,cbkj->cbi", upper_blocks, far_blocks, preferred_element_type=jnp.float32
        )
        transposed = col_weight[None] * far_blocks.astype(jnp.float32) - jnp.einsum(
            "bkij,cbi->cbkj", upper_blocks, own_block, preferred_element_type=jnp.float32
        )
        returned = jnp.zeros(window.shape, jnp.float32).at[:, local_index].add(transposed)
        summed = forward + returned[:, :shard_rows]
        for distance in range(1, REACH + 1):
            summed = summed + from_behind(
                returned[:, distance * shard_rows : (distance + 1) * shard_rows], "rows", distance
            )
        spread = lax.psum(summed, "cols")
        mapped = direction + 0.5 * spread.reshape(direction.shape)
        step_size = norm_now / lax.psum(jnp.sum(direction * mapped, axis=1), "rows")
        solution = solution + step_size[:, None] * direction
        residual = residual - step_size[:, None] * mapped
        if iteration + 1 < ITERS:
            norm_next = squares(residual)
            direction = residual + (norm_next / norm_now)[:, None] * direction
            norm_now = norm_next
    solution = lax.dynamic_slice_in_dim(solution, lax.axis_index("cols") * share, share, 0)
    residual = lax.dynamic_slice_in_dim(residual, lax.axis_index("cols") * share, share, 0)
    return (solution, residual)


def solution(mesh):
    in_specs = (P(None, "rows"), P("rows", "cols", None, None), P("rows", "cols"))
    out_specs = (P("cols", "rows"), P("cols", "rows"))
    return jax.shard_map(
        per_device, mesh=mesh, in_specs=in_specs, out_specs=out_specs, check_vma=False
    )
```

profile of v0, /device:TPU:8, one launch (start us, length us, event | category | flops | bytes accessed | tf_op | source)
XLA Modules:
  0.0 888.1 jit_solution(16670303994397478807)
XLA Ops:
  7.2 2.8 convert_element_type.22
  13.5 5.8 convert_reduce_fusion.1
  19.3 17.8 %collective-permute-done.1 = bf16[32,16384]{1,0:T(8,128)(2,1)} collective-permute-done((bf16[32,16384]{1,0:T(8,128)(2,1)}, bf16[32,16384]{1,0:T(8,128)(2,1)}, u32[]{:S(2)}, u32[]{:S(2)}) %collective-permute-start.1) | collective-permute-done | bytes 1048608 | tf_op jit(solution)/shard_map/ppermute | solution.py:13
  37.1 3.3 copy_bitcast_fusion.1
  40.4 4.0 gather_fusion
  44.5 8.5 bitcast_subtract_fusion.1
  53.0 3.5 broadcast.23.clone
  56.4 34.0 %scatter_fusion = f32[32,384,128]{2,0,1:T(8,128)} fusion(f32[32,384,128]{2,0,1:T(8,128)} %broadcast.23.clone, s32[256]{0:T(256)S(1)} %reshape.76, f32[256,32,128]{2,1,0:T(8,128)} %bitcast.94), kind=kCustom, calls=%fused_computation.2 | custom fusion | flops 1048576 | bytes 12583936 | tf_op jit(solution)/shard_map/scatter-add | solution.py:49
  90.4 2.8 fusion.21
  93.2 13.1 %collective-permute-start.2 = (f32[32,128,128]{2,0,1:T(8,128)S(1)}, f32[32,128,128]{2,0,1:T(8,128)S(1)}, u32[]{:S(2)}, u32[]{:S(2)}) collective-permute-start(f32[32,128,128]{2,0,1:T(8,128)S(1)} %get-tuple-element.17), channel_id=1, source_target_pairs={{0,4},{4,8},{8,12},{12,16},{16,20},{20,24},{24,28},{28,32},{32,36}... | collective-permute-start | bytes 6291464 | tf_op jit(solution)/shard_map/ppermute | solution.py:13
  106.3 3.4 collective-permute-start.3
  109.9 45.7 %collective-permute-done.3 = f32[32,128,128]{2,0,1:T(8,128)S(1)} collective-permute-done((f32[32,128,128]{2,0,1:T(8,128)S(1)}, f32[32,128,128]{2,0,1:T(8,128)S(1)}, u32[]{:S(2)}, u32[]{:S(2)}) %collective-permute-start.3) | collective-permute-done | bytes 2097184 | tf_op jit(solution)/shard_map/ppermute | solution.py:13
  155.7 8.3 fusion.3
  164.0 87.0 %all-reduce.4.cloned.1.call-done = f32[32,128,128]{2,0,1:T(8,128)} async-done(((f32[32,128,128]{2,0,1:T(8,128)}), f32[32,128,128]{2,0,1:T(8,128)}) %all-reduce.4.cloned.1.call-update) | async-done | bytes 2097168 | tf_op jit(solution)/shard_map/psum | solution.py:55
  251.1 2.1 multiply_reduce_fusion.2
  253.2 128.9 %all-reduce = (f32[32]{0:T(128)S(1)}, f32[32]{0:T(128)S(1)}) all-reduce(f32[32]{0:T(128)S(1)} %get-tuple-element.6, f32[32]{0:T(128)S(1)} %get-tuple-element.5), channel_id=1, replica_groups=mesh['rows'=64,'cols'=4] {'rows'}, use_global_device_ids=true, to_apply=%region_1.0 | all-reduce | flops 64 | bytes 512 | tf_op jit(solution)/shard_map/psum | solution.py:28
  382.1 3.4 multiply_reduce_fusion.1
  385.5 124.1 %psum.45 = f32[32]{0:T(128)S(1)} all-reduce(f32[32]{0:T(128)S(1)} %get-tuple-element.11), channel_id=1, replica_groups=mesh['rows'=64,'cols'=4] {'rows'}, use_global_device_ids=true, to_apply=%region_9.11 | all-reduce | flops 32 | bytes 256 | tf_op jit(solution)/shard_map/psum | solution.py:28
  509.6 3.3 fusion.19
  516.8 22.8 %collective-permute-done.5 = bf16[32,16384]{1,0:T(8,128)(2,1)S(1)} collective-permute-done((bf16[32,16384]{1,0:T(8,128)(2,1)S(1)}, bf16[32,16384]{1,0:T(8,128)(2,1)S(1)}, u32[]{:S(2)}, u32[]{:S(2)}) %collective-permute-start.5) | collective-permute-done | bytes 1048608 | tf_op jit(solution)/shard_map/ppermute | solution.py:13
  541.6 4.1 gather_fusion.1
  545.7 8.7 bitcast_subtract_fusion
  554.4 3.5 broadcast.23
  557.8 34.0 %scatter_fusion.1 = f32[32,384,128]{2,0,1:T(8,128)} fusion(f32[32,384,128]{2,0,1:T(8,128)} %broadcast.23, s32[256]{0:T(256)S(1)} %reshape.76, f32[256,32,128]{2,1,0:T(8,128)} %bitcast.93), kind=kCustom, calls=%fused_computation.3 | custom fusion | flops 1048576 | bytes 12583936 | tf_op jit(solution)/shard_map/scatter-add | solution.py:49
  591.8 2.8 fusion.20
  594.6 13.1 %collective-permute-start.6 = (f32[32,128,128]{2,0,1:T(8,128)S(1)}, f32[32,128,128]{2,0,1:T(8,128)S(1)}, u32[]{:S(2)}, u32[]{:S(2)}) collective-permute-start(f32[32,128,128]{2,0,1:T(8,128)S(1)} %get-tuple-element.15), channel_id=1, source_target_pairs={{0,4},{4,8},{8,12},{12,16},{16,20},{20,24},{24,28},{28,32},{32,36}... | collective-permute-start | bytes 6291464 | tf_op jit(solution)/shard_map/ppermute | solution.py:13
  611.3 44.0 %collective-permute-done.7 = f32[32,128,128]{2,0,1:T(8,128)S(1)} collective-permute-done((f32[32,128,128]{2,0,1:T(8,128)S(1)}, f32[32,128,128]{2,0,1:T(8,128)S(1)}, u32[]{:S(2)}, u32[]{:S(2)}) %collective-permute-start.7) | collective-permute-done | bytes 2097184 | tf_op jit(solution)/shard_map/ppermute | solution.py:13
  655.3 8.3 fusion.1
  663.7 82.1 %all-reduce.6.cloned.1.call-done = f32[32,128,128]{2,0,1:T(8,128)} async-done(((f32[32,128,128]{2,0,1:T(8,128)}), f32[32,128,128]{2,0,1:T(8,128)}) %all-reduce.6.cloned.1.call-update) | async-done | bytes 2097168 | tf_op jit(solution)/shard_map/psum | solution.py:55
  745.8 4.0 bitcast_add_fusion
  749.7 128.9 %psum.47 = f32[32]{0:T(128)S(1)} all-reduce(f32[32]{0:T(128)S(1)} %get-tuple-element.20), channel_id=1, replica_groups=mesh['rows'=64,'cols'=4] {'rows'}, use_global_device_ids=true, to_apply=%region_13.15 | all-reduce | flops 32 | bytes 256 | tf_op jit(solution)/shard_map/psum | solution.py:57
  878.8 2.5 dynamic-slice_subtract_fusion
  (35 shorter events, 13.4 us)
Async XLA Ops:
  7.2 5.9 copy-start
  7.2 5.5 copy-start.3
  7.2 243.9 %all-reduce.4.cloned.1.call-start = ((), (), s32[]{:S(2)}) async-start(), calls=%async_computation | async-start | bytes 4194304 | tf_op jit(solution)/shard_map/psum | solution.py:55
  10.0 27.1 %collective-permute-start.1 = (bf16[32,16384]{1,0:T(8,128)(2,1)}, bf16[32,16384]{1,0:T(8,128)(2,1)}, u32[]{:S(2)}, u32[]{:S(2)}) collective-permute-start(bf16[32,16384]{1,0:T(8,128)(2,1)} %convert_element_type.22), channel_id=1, source_target_pairs={{8,0},{12,4},{16,8},{20,12},{24,16},{28,20},{32,24},{36,28},{40,32... | collective-permute-start | bytes 3145736 | tf_op jit(solution)/shard_map/ppermute | solution.py:13
  11.3 25.8 %collective-permute-start = (bf16[32,16384]{1,0:T(8,128)(2,1)}, bf16[32,16384]{1,0:T(8,128)(2,1)}, u32[]{:S(2)}, u32[]{:S(2)}) collective-permute-start(bf16[32,16384]{1,0:T(8,128)(2,1)} %convert_element_type.22), channel_id=1, source_target_pairs={{4,0},{8,4},{12,8},{16,12},{20,16},{24,20},{28,24},{32,28},{36,32}... | collective-permute-start | bytes 3145736 | tf_op jit(solution)/shard_map/ppermute | solution.py:13
  90.4 65.3 %copy-start.1 = (bf16[256,32,128]{2,1,0:T(8,128)(2,1)S(1)}, bf16[256,32,128]{2,1,0:T(8,128)(2,1)}, u32[]{:S(2)}) copy-start(bf16[256,32,128]{2,1,0:T(8,128)(2,1)} %gather_fusion) | copy-start | bytes 6291460
  93.2 16.7 %collective-permute-start.2 = (f32[32,128,128]{2,0,1:T(8,128)S(1)}, f32[32,128,128]{2,0,1:T(8,128)S(1)}, u32[]{:S(2)}, u32[]{:S(2)}) collective-permute-start(f32[32,128,128]{2,0,1:T(8,128)S(1)} %get-tuple-element.17), channel_id=1, source_target_pairs={{0,4},{4,8},{8,12},{12,16},{16,20},{20,24},{24,28},{28,32},{32,36}... | collective-permute-start | bytes 6291464 | tf_op jit(solution)/shard_map/ppermute | solution.py:13
  106.3 49.4 %collective-permute-start.3 = (f32[32,128,128]{2,0,1:T(8,128)S(1)}, f32[32,128,128]{2,0,1:T(8,128)S(1)}, u32[]{:S(2)}, u32[]{:S(2)}) collective-permute-start(f32[32,128,128]{2,0,1:T(8,128)S(1)} %get-tuple-element.18), channel_id=1, source_target_pairs={{0,8},{4,12},{8,16},{12,20},{16,24},{20,28},{24,32},{28,36},{32,40... | collective-permute-start | bytes 6291464 | tf_op jit(solution)/shard_map/ppermute | solution.py:13
  164.0 581.8 %all-reduce.6.cloned.1.call-start = ((), (), s32[]{:S(2)}) async-start(), calls=%async_computation.1 | async-start | bytes 4194304 | tf_op jit(solution)/shard_map/psum | solution.py:55
  512.9 26.8 %collective-permute-start.5 = (bf16[32,16384]{1,0:T(8,128)(2,1)S(1)}, bf16[32,16384]{1,0:T(8,128)(2,1)S(1)}, u32[]{:S(2)}, u32[]{:S(2)}) collective-permute-start(bf16[32,16384]{1,0:T(8,128)(2,1)S(1)} %get-tuple-element.9), channel_id=1, source_target_pairs={{8,0},{12,4},{16,8},{20,12},{24,16},{28,20},{32,24},{36,28},{40,32... | collective-permute-start | bytes 3145736 | tf_op jit(solution)/shard_map/ppermute | solution.py:13
  514.2 25.5 %collective-permute-start.4 = (bf16[32,16384]{1,0:T(8,128)(2,1)S(1)}, bf16[32,16384]{1,0:T(8,128)(2,1)S(1)}, u32[]{:S(2)}, u32[]{:S(2)}) collective-permute-start(bf16[32,16384]{1,0:T(8,128)(2,1)S(1)} %get-tuple-element.9), channel_id=1, source_target_pairs={{4,0},{8,4},{12,8},{16,12},{20,16},{24,20},{28,24},{32,28},{36,32}... | collective-permute-start | bytes 3145736 | tf_op jit(solution)/shard_map/ppermute | solution.py:13
  591.8 63.5 %copy-start.2 = (bf16[256,32,128]{2,1,0:T(8,128)(2,1)S(1)}, bf16[256,32,128]{2,1,0:T(8,128)(2,1)}, u32[]{:S(2)}) copy-start(bf16[256,32,128]{2,1,0:T(8,128)(2,1)} %gather_fusion.1) | copy-start | bytes 6291460
  594.6 16.7 %collective-permute-start.6 = (f32[32,128,128]{2,0,1:T(8,128)S(1)}, f32[32,128,128]{2,0,1:T(8,128)S(1)}, u32[]{:S(2)}, u32[]{:S(2)}) collective-permute-start(f32[32,128,128]{2,0,1:T(8,128)S(1)} %get-tuple-element.15), channel_id=1, source_target_pairs={{0,4},{4,8},{8,12},{12,16},{16,20},{20,24},{24,28},{28,32},{32,36}... | collective-permute-start | bytes 6291464 | tf_op jit(solution)/shard_map/ppermute | solution.py:13
  607.7 47.6 %collective-permute-start.7 = (f32[32,128,128]{2,0,1:T(8,128)S(1)}, f32[32,128,128]{2,0,1:T(8,128)S(1)}, u32[]{:S(2)}, u32[]{:S(2)}) collective-permute-start(f32[32,128,128]{2,0,1:T(8,128)S(1)} %get-tuple-element.16), channel_id=1, source_target_pairs={{0,8},{4,12},{8,16},{12,20},{16,24},{20,28},{24,32},{28,36},{32,40... | collective-permute-start | bytes 6291464 | tf_op jit(solution)/shard_map/ppermute | solution.py:13
Sparse Core Ops, SparseCore 0:
  164.1 86.9 all-reduce.3
  663.8 81.9 all-reduce.5
where the time goes:
time: 889 us; the launch traced here: 888 us
  blocking collectives  382 us (43%)
  waiting for transfers between devices  302 us (34%)
  other arithmetic  97.2 us (11%)
  starting transfers between devices  36.6 us (4%)
  matrix products  33.8 us (4%)
  local copies, waits for them, and re-layouts  22.7 us (3%)
  between operations  14.2 us (2%)
    psum x2, blocking collectives, squares(): return lax.psum(jnp.sum(values * values, axis=1), 'rows')  253 us
    psum x2, waiting for transfers between devices, per_device(): spread = lax.psum(summed, 'cols')  169 us
    ppermute x8, waiting for transfers between devices, from_behind(): lax.ppermute(value, axis, [(source, source + steps) for source in range(i...  133 us
    psum x1, blocking collectives, per_device(): step_size = norm_now / lax.psum(jnp.sum(direction * mapped, axis=1), 'rows')  129 us
    scatter-add x2, other arithmetic, per_device(): jnp.zeros(window.shape, jnp.float32).at[:, local_index].add(transposed)  67.9 us
    ppermute x8, starting transfers between devices, from_behind(): lax.ppermute(value, axis, [(source, source + steps) for source in range(i...  36.5 us
  transfers between devices with their start and end apart: 10, of which 8 were waited for; matrix products, arithmetic and copies ran while one was open for 1% of the time, Pallas kernels for 0%

commit v1 on v0

--- a/solution.py
+++ b/solution.py
@@ -52,7 +52,7 @@
             summed = summed + from_behind(
                 returned[:, distance * shard_rows : (distance + 1) * shard_rows], "rows", distance
             )
-        spread = lax.psum(summed, "cols")
+        spread = lax.all_gather(summed, "cols").sum(axis=0)
         mapped = direction + 0.5 * spread.reshape(direction.shape)
         step_size = norm_now / lax.psum(jnp.sum(direction * mapped, axis=1), "rows")
         solution = solution + step_size[:, None] * direction

time: 889 us -> 949 us (1.067)
  waiting for transfers between devices: 302 us -> 350 us
  other arithmetic: 97.2 us -> 110 us
    all_gather x0 -> x2, waiting for transfers between devices: none -> 223 us  [per_device(): spread = lax.all_gather(summed, 'cols').sum(axis=0)]
    psum x2 -> x0, waiting for transfers between devices: 169 us -> none  [per_device(): spread = lax.psum(summed, 'cols')]
    reduce_sum x0 -> x2, other arithmetic: none -> 12.3 us  [per_device(): spread = lax.all_gather(summed, 'cols').sum(axis=0)]
  transfers between devices with their start and end apart: 10 -> 10, of which waited for: 8 -> 6; matrix products, arithmetic and copies ran while one was open for 1% -> 1% of each run, Pallas kernels for 0% -> 0%
where the time goes in v1:
time: 949 us; the launch traced here: 948 us
  blocking collectives  382 us (40%)
  waiting for transfers between devices  350 us (37%)
  other arithmetic  110 us (12%)
  starting transfers between devices  36.2 us (4%)
  matrix products  33.9 us (4%)
  local copies, waits for them, and re-layouts  22.7 us (2%)
  between operations  14.2 us (1%)
    psum x2, blocking collectives, squares(): return lax.psum(jnp.sum(values * values, axis=1), 'rows')  253 us
    all_gather x2, waiting for transfers between devices, per_device(): spread = lax.all_gather(summed, 'cols').sum(axis=0)  223 us
    psum x1, blocking collectives, per_device(): step_size = norm_now / lax.psum(jnp.sum(direction * mapped, axis=1), 'rows')  129 us
    ppermute x8, waiting for transfers between devices, from_behind(): lax.ppermute(value, axis, [(source, source + steps) for source in range(i...  127 us
    scatter-add x2, other arithmetic, per_device(): jnp.zeros(window.shape, jnp.float32).at[:, local_index].add(transposed)  67.9 us
    ppermute x8, starting transfers between devices, from_behind(): lax.ppermute(value, axis, [(source, source + steps) for source in range(i...  36 us
  transfers between devices with their start and end apart: 10, of which 6 were waited for; matrix products, arithmetic and copies ran while one was open for 1% of the time, Pallas kernels for 0%

profile of v1, /device:TPU:8, one launch (start us, length us, event | category | flops | bytes accessed | tf_op | source)
XLA Modules:
  0.0 947.9 jit_solution(2310999546415678535)
XLA Ops:
  7.2 2.8 convert_element_type.22
  13.5 5.8 convert_reduce_fusion.1
  19.3 17.8 %collective-permute-done.1 = bf16[32,16384]{1,0:T(8,128)(2,1)} collective-permute-done((bf16[32,16384]{1,0:T(8,128)(2,1)}, bf16[32,16384]{1,0:T(8,128)(2,1)}, u32[]{:S(2)}, u32[]{:S(2)}) %collective-permute-start.1) | collective-permute-done | bytes 1048608 | tf_op jit(solution)/shard_map/ppermute | solution.py:13
  37.1 3.3 copy_bitcast_fusion.1
  40.4 4.0 gather_fusion
  44.5 8.5 bitcast_subtract_fusion.1
  53.0 3.5 broadcast.23.clone
  56.4 34.0 %scatter_fusion = f32[32,384,128]{2,0,1:T(8,128)} fusion(f32[32,384,128]{2,0,1:T(8,128)} %broadcast.23.clone, s32[256]{0:T(256)S(1)} %reshape.78, f32[256,32,128]{2,1,0:T(8,128)} %bitcast.96), kind=kCustom, calls=%fused_computation.2 | custom fusion | flops 1048576 | bytes 12583936 | tf_op jit(solution)/shard_map/scatter-add | solution.py:49
  90.4 2.8 fusion.21
  93.2 12.8 %collective-permute-start.3 = (f32[32,128,128]{2,0,1:T(8,128)S(1)}, f32[32,128,128]{2,0,1:T(8,128)S(1)}, u32[]{:S(2)}, u32[]{:S(2)}) collective-permute-start(f32[32,128,128]{2,0,1:T(8,128)S(1)} %get-tuple-element.18), channel_id=1, source_target_pairs={{0,8},{4,12},{8,16},{12,20},{16,24},{20,28},{24,32},{28,36},{32,40... | collective-permute-start | bytes 6291464 | tf_op jit(solution)/shard_map/ppermute | solution.py:13
  106.0 3.5 collective-permute-start.2
  109.6 41.6 %collective-permute-done.3 = f32[32,128,128]{2,0,1:T(8,128)S(1)} collective-permute-done((f32[32,128,128]{2,0,1:T(8,128)S(1)}, f32[32,128,128]{2,0,1:T(8,128)S(1)}, u32[]{:S(2)}, u32[]{:S(2)}) %collective-permute-start.3) | collective-permute-done | bytes 2097184 | tf_op jit(solution)/shard_map/ppermute | solution.py:13
  151.2 8.3 fusion.3
  159.7 114.9 %all-gather.5.cloned.1.call-done = f32[128,128,128]{2,0,1:T(8,128)} async-done(((f32[32,128,128]{2,0,1:T(8,128)}), f32[128,128,128]{2,0,1:T(8,128)}) %all-gather.5.cloned.1.call-update) | async-done | bytes 8388624 | tf_op jit(solution)/shard_map/all_gather | solution.py:55
  274.7 6.2 reduce_sum.75
  282.9 128.9 %all-reduce = (f32[32]{0:T(128)S(1)}, f32[32]{0:T(128)S(1)}) all-reduce(f32[32]{0:T(128)S(1)} %get-tuple-element.6, f32[32]{0:T(128)S(1)} %get-tuple-element.5), channel_id=1, replica_groups=mesh['rows'=64,'cols'=4] {'rows'}, use_global_device_ids=true, to_apply=%region_1.0 | all-reduce | flops 64 | bytes 512 | tf_op jit(solution)/shard_map/psum | solution.py:28
  411.8 3.4 multiply_reduce_fusion.1
  415.3 124.1 %psum.30 = f32[32]{0:T(128)S(1)} all-reduce(f32[32]{0:T(128)S(1)} %get-tuple-element.11), channel_id=1, replica_groups=mesh['rows'=64,'cols'=4] {'rows'}, use_global_device_ids=true, to_apply=%region_9.11 | all-reduce | flops 32 | bytes 256 | tf_op jit(solution)/shard_map/psum | solution.py:28
  539.3 3.3 fusion.19
  546.4 23.0 %collective-permute-done.5 = bf16[32,16384]{1,0:T(8,128)(2,1)S(1)} collective-permute-done((bf16[32,16384]{1,0:T(8,128)(2,1)S(1)}, bf16[32,16384]{1,0:T(8,128)(2,1)S(1)}, u32[]{:S(2)}, u32[]{:S(2)}) %collective-permute-start.5) | collective-permute-done | bytes 1048608 | tf_op jit(solution)/shard_map/ppermute | solution.py:13
  571.3 4.1 gather_fusion.1
  575.4 8.7 bitcast_subtract_fusion
  584.1 3.5 broadcast.23
  587.5 34.0 %scatter_fusion.1 = f32[32,384,128]{2,0,1:T(8,128)} fusion(f32[32,384,128]{2,0,1:T(8,128)} %broadcast.23, s32[256]{0:T(256)S(1)} %reshape.78, f32[256,32,128]{2,1,0:T(8,128)} %bitcast.95), kind=kCustom, calls=%fused_computation.3 | custom fusion | flops 1048576 | bytes 12583936 | tf_op jit(solution)/shard_map/scatter-add | solution.py:49
  621.5 2.8 fusion.20
  624.3 12.8 %collective-permute-start.7 = (f32[32,128,128]{2,0,1:T(8,128)S(1)}, f32[32,128,128]{2,0,1:T(8,128)S(1)}, u32[]{:S(2)}, u32[]{:S(2)}) collective-permute-start(f32[32,128,128]{2,0,1:T(8,128)S(1)} %get-tuple-element.16), channel_id=1, source_target_pairs={{0,8},{4,12},{8,16},{12,20},{16,24},{20,28},{24,32},{28,36},{32,40... | collective-permute-start | bytes 6291464 | tf_op jit(solution)/shard_map/ppermute | solution.py:13
  638.8 44.2 %collective-permute-done.7 = f32[32,128,128]{2,0,1:T(8,128)S(1)} collective-permute-done((f32[32,128,128]{2,0,1:T(8,128)S(1)}, f32[32,128,128]{2,0,1:T(8,128)S(1)}, u32[]{:S(2)}, u32[]{:S(2)}) %collective-permute-start.7) | collective-permute-done | bytes 2097184 | tf_op jit(solution)/shard_map/ppermute | solution.py:13
  683.0 8.4 fusion.1
  691.5 108.0 %all-gather.7.cloned.1.call-done = f32[128,128,128]{2,0,1:T(8,128)} async-done(((f32[32,128,128]{2,0,1:T(8,128)}), f32[128,128,128]{2,0,1:T(8,128)}) %all-gather.7.cloned.1.call-update) | async-done | bytes 8388624 | tf_op jit(solution)/shard_map/all_gather | solution.py:55
  799.5 6.2 reduce_sum.78
  805.7 4.0 bitcast_add_fusion
  809.6 128.9 %psum.31 = f32[32]{0:T(128)S(1)} all-reduce(f32[32]{0:T(128)S(1)} %get-tuple-element.20), channel_id=1, replica_groups=mesh['rows'=64,'cols'=4] {'rows'}, use_global_device_ids=true, to_apply=%region_13.15 | all-reduce | flops 32 | bytes 256 | tf_op jit(solution)/shard_map/psum | solution.py:57
  (37 shorter events, 15.8 us)
Async XLA Ops:
  7.2 5.9 copy-start
  7.2 5.5 copy-start.3
  7.2 267.5 %all-gather.5.cloned.1.call-start = ((), (), s32[]{:S(2)}) async-start(), calls=%async_computation | async-start | bytes 10485760 | tf_op jit(solution)/shard_map/all_gather | solution.py:55
  10.0 27.1 %collective-permute-start.1 = (bf16[32,16384]{1,0:T(8,128)(2,1)}, bf16[32,16384]{1,0:T(8,128)(2,1)}, u32[]{:S(2)}, u32[]{:S(2)}) collective-permute-start(bf16[32,16384]{1,0:T(8,128)(2,1)} %convert_element_type.22), channel_id=1, source_target_pairs={{8,0},{12,4},{16,8},{20,12},{24,16},{28,20},{32,24},{36,28},{40,32... | collective-permute-start | bytes 3145736 | tf_op jit(solution)/shard_map/ppermute | solution.py:13
  11.3 25.8 %collective-permute-start = (bf16[32,16384]{1,0:T(8,128)(2,1)}, bf16[32,16384]{1,0:T(8,128)(2,1)}, u32[]{:S(2)}, u32[]{:S(2)}) collective-permute-start(bf16[32,16384]{1,0:T(8,128)(2,1)} %convert_element_type.22), channel_id=1, source_target_pairs={{4,0},{8,4},{12,8},{16,12},{20,16},{24,20},{28,24},{32,28},{36,32}... | collective-permute-start | bytes 3145736 | tf_op jit(solution)/shard_map/ppermute | solution.py:13
  90.4 60.7 %copy-start.1 = (bf16[256,32,128]{2,1,0:T(8,128)(2,1)S(1)}, bf16[256,32,128]{2,1,0:T(8,128)(2,1)}, u32[]{:S(2)}) copy-start(bf16[256,32,128]{2,1,0:T(8,128)(2,1)} %gather_fusion) | copy-start | bytes 6291460
  93.2 57.9 %collective-permute-start.3 = (f32[32,128,128]{2,0,1:T(8,128)S(1)}, f32[32,128,128]{2,0,1:T(8,128)S(1)}, u32[]{:S(2)}, u32[]{:S(2)}) collective-permute-start(f32[32,128,128]{2,0,1:T(8,128)S(1)} %get-tuple-element.18), channel_id=1, source_target_pairs={{0,8},{4,12},{8,16},{12,20},{16,24},{20,28},{24,32},{28,36},{32,40... | collective-permute-start | bytes 6291464 | tf_op jit(solution)/shard_map/ppermute | solution.py:13
  106.0 45.1 %collective-permute-start.2 = (f32[32,128,128]{2,0,1:T(8,128)S(1)}, f32[32,128,128]{2,0,1:T(8,128)S(1)}, u32[]{:S(2)}, u32[]{:S(2)}) collective-permute-start(f32[32,128,128]{2,0,1:T(8,128)S(1)} %get-tuple-element.17), channel_id=1, source_target_pairs={{0,4},{4,8},{8,12},{12,16},{16,20},{20,24},{24,28},{28,32},{32,36}... | collective-permute-start | bytes 6291464 | tf_op jit(solution)/shard_map/ppermute | solution.py:13
  159.5 640.0 %all-gather.7.cloned.1.call-start = ((), (), s32[]{:S(2)}) async-start(), calls=%async_computation.1 | async-start | bytes 10485760 | tf_op jit(solution)/shard_map/all_gather | solution.py:55
  542.6 26.8 %collective-permute-start.5 = (bf16[32,16384]{1,0:T(8,128)(2,1)S(1)}, bf16[32,16384]{1,0:T(8,128)(2,1)S(1)}, u32[]{:S(2)}, u32[]{:S(2)}) collective-permute-start(bf16[32,16384]{1,0:T(8,128)(2,1)S(1)} %get-tuple-element.9), channel_id=1, source_target_pairs={{8,0},{12,4},{16,8},{20,12},{24,16},{28,20},{32,24},{36,28},{40,32... | collective-permute-start | bytes 3145736 | tf_op jit(solution)/shard_map/ppermute | solution.py:13
  543.9 25.5 %collective-permute-start.4 = (bf16[32,16384]{1,0:T(8,128)(2,1)S(1)}, bf16[32,16384]{1,0:T(8,128)(2,1)S(1)}, u32[]{:S(2)}, u32[]{:S(2)}) collective-permute-start(bf16[32,16384]{1,0:T(8,128)(2,1)S(1)} %get-tuple-element.9), channel_id=1, source_target_pairs={{4,0},{8,4},{12,8},{16,12},{20,16},{24,20},{28,24},{32,28},{36,32}... | collective-permute-start | bytes 3145736 | tf_op jit(solution)/shard_map/ppermute | solution.py:13
  621.5 61.5 %copy-start.2 = (bf16[256,32,128]{2,1,0:T(8,128)(2,1)S(1)}, bf16[256,32,128]{2,1,0:T(8,128)(2,1)}, u32[]{:S(2)}) copy-start(bf16[256,32,128]{2,1,0:T(8,128)(2,1)} %gather_fusion.1) | copy-start | bytes 6291460
  624.3 58.7 %collective-permute-start.7 = (f32[32,128,128]{2,0,1:T(8,128)S(1)}, f32[32,128,128]{2,0,1:T(8,128)S(1)}, u32[]{:S(2)}, u32[]{:S(2)}) collective-permute-start(f32[32,128,128]{2,0,1:T(8,128)S(1)} %get-tuple-element.16), channel_id=1, source_target_pairs={{0,8},{4,12},{8,16},{12,20},{16,24},{20,28},{24,32},{28,36},{32,40... | collective-permute-start | bytes 6291464 | tf_op jit(solution)/shard_map/ppermute | solution.py:13
  637.1 45.9 %collective-permute-start.6 = (f32[32,128,128]{2,0,1:T(8,128)S(1)}, f32[32,128,128]{2,0,1:T(8,128)S(1)}, u32[]{:S(2)}, u32[]{:S(2)}) collective-permute-start(f32[32,128,128]{2,0,1:T(8,128)S(1)} %get-tuple-element.15), channel_id=1, source_target_pairs={{0,4},{4,8},{8,12},{12,16},{16,20},{20,24},{24,28},{28,32},{32,36}... | collective-permute-start | bytes 6291464 | tf_op jit(solution)/shard_map/ppermute | solution.py:13
Sparse Core Ops, SparseCore 0:
  159.6 114.9 all-gather.4
  691.5 107.9 all-gather.6
